TPU v7x, 32 devices: a whole 2x2x4 slice. The times are simulated.
32 devices in a mesh: rows: 4 (over z), pos: 8 (over y, x, core).
Axes of the slice: x: 2, y: 2, z: 4, core: 2. Of those that a mesh axis runs over, the one named last changes fastest.
Arguments:
- tokens: bfloat16 [16, 2048, 768], P('rows', 'pos'), may hold values from -6 to 6
- segment_ids: int32 [16, 2048], P('rows', 'pos'), may hold values from 0 to 2, as said below
- group_sizes: int32 [16, 2], P('rows'), may hold values from 4 to 16, as said below
- prefix_lens: int32 [16, 2], P('rows'), may hold values from 1 to 768, as said below
- solution_lens: int32 [16, 2, 16], P('rows'), may hold values from 0 to 657, as said below
- padding_counts: int32 [16], P('rows'), may hold values from 0 to 128, as said below
- attn_gain: bfloat16 [768], replicated, may hold values from 0.5 to 1.5
- attn_shift: bfloat16 [768], replicated, may hold values from -1 to 1
- w_qkv: bfloat16 [768, 2304], replicated, may hold values from -0.21875 to 0.21875
- query_bias: bfloat16 [768], replicated, may hold values from -2.5 to 2.5
- value_bias: bfloat16 [768], replicated, may hold values from -1.5 to 1.5
- w_out: bfloat16 [768, 768], replicated, may hold values from -0.875 to 0.875
- out_bias: bfloat16 [768], replicated, may hold values from -1.5 to 1.5
- ffn_gain: bfloat16 [768], replicated, may hold values from 0.5 to 1.5
- ffn_shift: bfloat16 [768], replicated, may hold values from -1 to 1
- w_up: bfloat16 [768, 3072], replicated, may hold values from -0.21875 to 0.21875
- up_bias: bfloat16 [3072], replicated, may hold values from -2.5 to 2.5
- w_down: bfloat16 [3072, 768], replicated, may hold values from -0.109375 to 0.109375
- down_bias: bfloat16 [768], replicated, may hold values from -1.5 to 1.5
- cotangent: bfloat16 [16, 2048, 768], P('rows', 'pos'), may hold values from -6 to 6
Outputs:
- layer_out: bfloat16 [16, 2048, 768], P('rows', 'pos')
- tokens_grad: bfloat16 [16, 2048, 768], P('rows', 'pos')
- grad_attn_gain: float32 [768], replicated
- grad_attn_shift: float32 [768], replicated
- grad_w_qkv: float32 [768, 2304], replicated
- grad_query_bias: float32 [768], replicated
- grad_value_bias: float32 [768], replicated
- grad_w_out: float32 [768, 768], replicated
- grad_out_bias: float32 [768], replicated
- grad_ffn_gain: float32 [768], replicated
- grad_ffn_shift: float32 [768], replicated
- grad_w_up: float32 [768, 3072], replicated
- grad_up_bias: float32 [3072], replicated
- grad_w_down: float32 [3072, 768], replicated
- grad_down_bias: float32 [768], replicated
Inputs may be any that keep to these rules, and one draw needn't show every extreme that they name: `group_sizes`: each group holds this many solutions. `solution_lens`: A group's solutions at index group_sizes or more have length 0, the others 1 or more. `prefix_lens`: each prefix has 1 or more positions. `segment_ids`: A row holds group 0 (its prefix, then its solutions in order), then group 1, then padding_counts padding positions marked 2; together exactly 2048 positions. `padding_counts`: the row's positions after both groups.
All inputs are finite; a program needn't handle non-finite values.
Results may differ from a plain program's by a relative error of at most 0.012.
Values may be sent and summed in bfloat16 or wider, within the bound.
No kernel may reach another device: no remote copies, remote signals or barrier semaphores. Data moves between devices by JAX's collectives and lax.ppermute only.
A program may use at most 448 MiB of HBM per device.

v0:
```python
import math
import jax
import jax.numpy as jnp
from jax import lax
from jax.sharding import PartitionSpec as P

HEAD_DIM = 64
EPS = 1e-05
NEG = -1e30
GELU_C = 0.7978845608028654


def layer_norm(values, gain, shift):
    center = values - jnp.mean(values, axis=-1, keepdims=True)
    spread = jnp.mean(center * center, axis=-1, keepdims=True)
    return center * lax.rsqrt(spread + EPS) * gain + shift


def gelu_tanh(values):
    return 0.5 * values * (1.0 + jnp.tanh(GELU_C * (values + 0.044715 * values * values * values)))


def classes(places, segments, sizes_row, prefix_row, lens_row, padding_row, length):
    slots = jnp.arange(lens_row.shape[-1], dtype=jnp.int32)
    kept_lens = jnp.where(slots[None, None, :] < sizes_row[:, :, None], lens_row, 0)
    solution_ends = jnp.cumsum(kept_lens, axis=-1)
    totals = prefix_row + solution_ends[:, :, -1]
    starts = jnp.cumsum(totals, axis=-1) - totals
    groups = jnp.arange(sizes_row.shape[-1], dtype=jnp.int32)
    member = segments[:, :, None] == groups[None, None, :]
    group_start = jnp.sum(jnp.where(member, starts[:, None, :], 0), axis=-1)
    prefix_here = jnp.sum(jnp.where(member, prefix_row[:, None, :], 0), axis=-1)
    inside = places[None, :] - group_start - prefix_here
    passed = jnp.where(
        member[:, :, :, None], inside[:, :, None, None] >= solution_ends[:, None, :, :], False
    )
    passed_count = jnp.sum(passed.astype(jnp.int32), axis=(2, 3))
    branch = jnp.where(inside < 0, -1, passed_count)
    padded = places[None, :] >= length - padding_row[:, None]
    class_id = jnp.where(padded, -1, segments)
    branch = jnp.where(padded, -2, branch)
    return (class_id, branch)


def visible(query_class, query_branch, query_places, key_class, key_branch, key_places):
    same = query_class[:, :, None] == key_class[:, None, :]
    causal = key_places[None, None, :] <= query_places[None, :, None]
    shared = (key_branch[:, None, :] == -1) | (key_branch[:, None, :] == query_branch[:, :, None])
    return same & causal & shared


def heads_first(values):
    return values.reshape(
        values.shape[0], values.shape[1], values.shape[2] // HEAD_DIM, HEAD_DIM
    ).transpose(2, 0, 1, 3)


def heads_last(values):
    return values.transpose(1, 2, 0, 3).reshape(
        values.shape[1], values.shape[2], values.shape[0] * values.shape[3]
    )


def head_scores(query_head, key_head, allowed, score_scale):
    product = (
        jnp.einsum("rqe,rke->rqk", query_head, key_head, preferred_element_type=jnp.float32)
        * score_scale
    )
    return jnp.where(allowed, product, NEG)


def outer_sum(left, right):
    return lax.dot_general(
        left.reshape(-1, left.shape[-1]),
        right.reshape(-1, right.shape[-1]),
        (((0,), (0,)), ((), ())),
        preferred_element_type=jnp.float32,
    )


def back_through(grad, weight):
    return jnp.einsum("rpo,io->rpi", grad, weight, preferred_element_type=jnp.float32)


def column_sum(values):
    return jnp.sum(values, axis=(0, 1), dtype=jnp.float32)


def per_device(
    tokens,
    segment_ids,
    group_sizes,
    prefix_lens,
    solution_lens,
    padding_counts,
    attn_gain,
    attn_shift,
    w_qkv,
    query_bias,
    value_bias,
    w_out,
    out_bias,
    ffn_gain,
    ffn_shift,
    w_up,
    up_bias,
    w_down,
    down_bias,
    cotangent,
):
    row_count, local_len, model_width = tokens.shape
    row_len = local_len * lax.axis_size("pos")
    score_scale = 1.0 / math.sqrt(HEAD_DIM)
    local_places = lax.axis_index("pos") * local_len + jnp.arange(local_len, dtype=jnp.int32)
    all_places = jnp.arange(row_len, dtype=jnp.int32)
    inputs = tokens.astype(jnp.float32)
    normed_one, norm_one_pull = jax.vjp(
        layer_norm, inputs, attn_gain.astype(jnp.float32), attn_shift.astype(jnp.float32)
    )
    act_one = normed_one.astype(jnp.bfloat16)
    projected = jnp.dot(act_one, w_qkv, preferred_element_type=jnp.float32)
    queries = (projected[..., :model_width] + query_bias.astype(jnp.float32)).astype(jnp.bfloat16)
    keys_local = projected[..., model_width : 2 * model_width].astype(jnp.bfloat16)
    values_local = (projected[..., 2 * model_width :] + value_bias.astype(jnp.float32)).astype(
        jnp.bfloat16
    )
    segment_wire = segment_ids.astype(jnp.bfloat16)
    keys_all, values_all, segment_all = (
        lax.all_gather(keys_local, "pos", axis=1, tiled=True),
        lax.all_gather(values_local, "pos", axis=1, tiled=True),
        lax.all_gather(segment_wire, "pos", axis=1, tiled=True),
    )
    query_class, query_branch = classes(
        local_places, segment_ids, group_sizes, prefix_lens, solution_lens, padding_counts, row_len
    )
    key_class, key_branch = classes(
        all_places,
        segment_all.astype(jnp.int32),
        group_sizes,
        prefix_lens,
        solution_lens,
        padding_counts,
        row_len,
    )
    allowed = visible(query_class, query_branch, local_places, key_class, key_branch, all_places)

    def forward_head(triple):
        query_head, key_head, value_head = triple
        scores = head_scores(query_head, key_head, allowed, score_scale)
        top_head = jnp.max(scores, axis=-1)
        weights = jnp.exp(scores - top_head[..., None])
        total_head = jnp.sum(weights, axis=-1)
        probs_low = (weights / total_head[..., None]).astype(jnp.bfloat16)
        mixed_head = jnp.einsum(
            "rqk,rke->rqe", probs_low, value_head, preferred_element_type=jnp.float32
        )
        return (mixed_head, top_head, total_head)

    queries_heads = heads_first(queries)
    mixed_heads, top, total = lax.map(
        forward_head, (queries_heads, heads_first(keys_all), heads_first(values_all))
    )
    mixed_low = heads_last(mixed_heads).astype(jnp.bfloat16)
    resid = inputs + (
        jnp.dot(mixed_low, w_out, preferred_element_type=jnp.float32) + out_bias.astype(jnp.float32)
    )
    normed_two, norm_two_pull = jax.vjp(
        layer_norm, resid, ffn_gain.astype(jnp.float32), ffn_shift.astype(jnp.float32)
    )
    act_two = normed_two.astype(jnp.bfloat16)
    upper = jnp.dot(act_two, w_up, preferred_element_type=jnp.float32) + up_bias.astype(jnp.float32)
    hidden_full, gelu_pull = jax.vjp(gelu_tanh, upper)
    hidden = hidden_full.astype(jnp.bfloat16)
    layer_out = (
        resid
        + (
            jnp.dot(hidden, w_down, preferred_element_type=jnp.float32)
            + down_bias.astype(jnp.float32)
        )
    ).astype(jnp.bfloat16)
    grad_out = cotangent.astype(jnp.float32)
    grad_w_down = outer_sum(hidden, cotangent)
    grad_down_bias = column_sum(grad_out)
    (grad_upper_full,) = gelu_pull(back_through(cotangent, w_down))
    grad_upper = grad_upper_full.astype(jnp.bfloat16)
    grad_w_up = outer_sum(act_two, grad_upper)
    grad_up_bias = column_sum(grad_upper)
    grad_resid_norm, grad_ffn_gain, grad_ffn_shift = norm_two_pull(back_through(grad_upper, w_up))
    grad_resid = grad_out + grad_resid_norm
    grad_attn = grad_resid.astype(jnp.bfloat16)
    grad_w_out = outer_sum(mixed_low, grad_attn)
    grad_out_bias = column_sum(grad_attn)
    grad_mixed = back_through(grad_attn, w_out).astype(jnp.bfloat16)
    keys_again, values_again = (
        lax.all_gather(keys_local, "pos", axis=1, tiled=True),
        lax.all_gather(values_local, "pos", axis=1, tiled=True),
    )
    grad_mixed_heads = heads_first(grad_mixed)

    def backward_head(items):
        query_head, key_head, value_head, grad_head, top_head, total_head = items
        scores = head_scores(query_head, key_head, allowed, score_scale)
        probs = jnp.exp(scores - top_head[..., None]) / total_head[..., None]
        grad_probs = jnp.einsum(
            "rqe,rke->rqk", grad_head, value_head, preferred_element_type=jnp.float32
        )
        delta_head = jnp.sum(probs * grad_probs, axis=-1)
        grad_scores = (probs * (grad_probs - delta_head[..., None])).astype(jnp.bfloat16)
        query_grad = (
            jnp.einsum("rqk,rke->rqe", grad_scores, key_head, preferred_element_type=jnp.float32)
            * score_scale
        ).astype(jnp.bfloat16)
        key_term = (
            jnp.einsum("rqk,rqe->rke", grad_scores, query_head, preferred_element_type=jnp.float32)
            * score_scale
        )
        value_term = jnp.einsum(
            "rqk,rqe->rke",
            probs.astype(jnp.bfloat16),
            grad_head,
            preferred_element_type=jnp.float32,
        )
        return (query_grad, key_term, value_term, delta_head)

    query_heads_grad, key_heads, value_heads, delta = lax.map(
        backward_head,
        (
            queries_heads,
            heads_first(keys_again),
            heads_first(values_again),
            grad_mixed_heads,
            top,
            total,
        ),
    )
    key_sum, value_sum = (
        lax.psum_scatter(heads_last(key_heads), "pos", scatter_dimension=1, tiled=True),
        lax.psum_scatter(heads_last(value_heads), "pos", scatter_dimension=1, tiled=True),
    )
    grad_queries = heads_last(query_heads_grad)
    grad_keys = key_sum.astype(jnp.bfloat16)
    grad_values = value_sum.astype(jnp.bfloat16)
    grad_project = jnp.concatenate([grad_queries, grad_keys, grad_values], axis=-1)
    grad_w_qkv = outer_sum(act_one, grad_project)
    grad_query_bias = column_sum(grad_queries)
    grad_value_bias = column_sum(grad_values)
    grad_input_norm, grad_attn_gain, grad_attn_shift = norm_one_pull(
        back_through(grad_project, w_qkv)
    )
    tokens_grad = (grad_resid + grad_input_norm).astype(jnp.bfloat16)
    summed = lax.psum(
        (
            grad_attn_gain,
            grad_attn_shift,
            grad_w_qkv,
            grad_query_bias,
            grad_value_bias,
            grad_w_out,
            grad_out_bias,
            grad_ffn_gain,
            grad_ffn_shift,
            grad_w_up,
            grad_up_bias,
            grad_w_down,
            grad_down_bias,
        ),
        ("rows", "pos"),
    )
    return (
        layer_out,
        tokens_grad,
        summed[0],
        summed[1],
        summed[2],
        summed[3],
        summed[4],
        summed[5],
        summed[6],
        summed[7],
        summed[8],
        summed[9],
        summed[10],
        summed[11],
        summed[12],
    )


def solution(mesh):
    in_specs = (
        P("rows", "pos", None),
        P("rows", "pos"),
        P("rows", None),
        P("rows", None),
        P("rows", None, None),
        P("rows"),
        P(),
        P(),
        P(),
        P(),
        P(),
        P(),
        P(),
        P(),
        P(),
        P(),
        P(),
        P(),
        P(),
        P("rows", "pos", None),
    )
    out_specs = (
        P("rows", "pos", None),
        P("rows", "pos", None),
        P(),
        P(),
        P(),
        P(),
        P(),
        P(),
        P(),
        P(),
        P(),
        P(),
        P(),
        P(),
        P(),
    )
    return jax.shard_map(
        per_device, mesh=mesh, in_specs=in_specs, out_specs=out_specs, check_vma=False
    )
```

profile of v0, /device:TPU:0, one launch (start us, length us, event | category | flops | bytes accessed | tf_op | source)
XLA Modules:
  0.0 1607.0 jit_solution(12968616290820048877)
XLA Ops:
  39.0 10.9 all_gather.12
  60.9 38.5 %all-gather.5.cloned.1.call-done = bf16[4,2048,768]{2,1,0:T(8,128)(2,1)} async-done(((bf16[4,256,768]{2,1,0:T(8,128)(2,1)}), bf16[4,2048,768]{2,1,0:T(8,128)(2,1)}) %all-gather.5.cloned.1.call-update) | async-done | bytes 12582928 | tf_op jit(solution)/shard_map/all_gather | solution.py:130
  99.3 16.5 %copy.82 = bf16[4,2048,768]{1,2,0:T(8,128)(2,1)} copy(bf16[4,2048,768]{2,1,0:T(8,128)(2,1)} %all-gather.5.cloned.1.call-done) | data formatting | bytes 25165824 | tf_op jit(solution)/shard_map/all_gather | solution.py:130
  115.8 10.7 copy.89
  126.5 47.4 %all-gather.3.cloned.1.call-done = bf16[4,2048,768]{2,1,0:T(8,128)(2,1)} async-done(((bf16[4,256,768]{2,1,0:T(8,128)(2,1)}), bf16[4,2048,768]{2,1,0:T(8,128)(2,1)}) %all-gather.3.cloned.1.call-update) | async-done | bytes 12582928 | tf_op jit(solution)/shard_map/all_gather | solution.py:129
  173.8 16.0 copy.81
  189.9 10.7 copy.88
  200.6 127.0 %while.30 = (s32[]{:T(128)}, bf16[12,4,256,64]{2,3,0,1:T(8,128)(2,1)}, f32[12,4,256]{2,1,0:T(4,128)}, f32[12,4,256]{2,1,0:T(4,128)}, bf16[12,4,256,64]{2,3,1,0:T...) while((s32[]{:T(128)}, ...), condition=%wide.region_13.14_spmd.clone, body=%wide.region_10.13_spmd.clone.sunk | while | flops 564131840 | bytes 28301456 | solution.py:160
  332.2 8.5 fusion.65
  340.7 17.8 %convert_reduce_fusion = (f32[3072]{0:T(1024)}, bf16[4,256,3072]{2,1,0:T(8,128)(2,1)S(1)}) fusion(bf16[4,256,768]{2,1,0:T(8,128)(2,1)S(1)} %copy-done.12, bf16[3072,768]{1,0:T(8,128)(2,1)} %param.41, f32[4,256,3072]{2,1,0:T(8,128)} %fusion.65, f32[3072]{0:T(1024)S(1)} %copy-done.50), kind=kOutput, calls=%fused_computation.65 | convolution fusion | flops 4916769792 | bytes 25190400 | tf_op jit(solution)/shard_map/rpo,io->rpi/dot_general | solution.py:82
  358.5 6.1 multiply_reduce_fusion.1
  374.3 422.0 %while.31 = (s32[]{:T(128)}, bf16[12,4,256,64]{2,3,0,1:T(8,128)(2,1)}, f32[12,4,2048,64]{2,3,0,1:T(8,128)}, f32[12,4,2048,64]{2,3,0,1:T(8,128)}, bf16[12,4,256,6...) while((s32[]{:T(128)}, ...), condition=%wide.region_20.21_spmd.clone, body=%wide.region_18.20_spmd.clone.sunk | while | flops 1374288896 | bytes 124245304 | solution.py:225
  377.7 9.8 multiply_reduce_fusion.5
  387.5 8.5 multiply_convert_fusion.5
  412.8 9.8 multiply_reduce_fusion.5
  422.6 8.5 multiply_convert_fusion.5
  447.9 9.8 multiply_reduce_fusion.5
  457.7 8.5 multiply_convert_fusion.5
  483.1 9.8 multiply_reduce_fusion.5
  492.8 8.5 multiply_convert_fusion.5
  518.3 9.8 multiply_reduce_fusion.5
  528.1 8.5 multiply_convert_fusion.5
  553.5 9.8 multiply_reduce_fusion.5
  563.3 8.5 multiply_convert_fusion.5
  588.7 9.8 multiply_reduce_fusion.5
  598.5 8.5 multiply_convert_fusion.5
  624.0 9.8 multiply_reduce_fusion.5
  633.8 8.5 multiply_convert_fusion.5
  659.1 9.8 multiply_reduce_fusion.5
  668.9 8.5 multiply_convert_fusion.5
  694.3 9.8 multiply_reduce_fusion.5
  704.0 8.5 multiply_convert_fusion.5
  729.4 9.8 multiply_reduce_fusion.5
  739.2 8.5 multiply_convert_fusion.5
  764.7 9.8 multiply_reduce_fusion.5
  774.5 8.5 multiply_convert_fusion.5
  796.4 24.7 %copy.99 = f32[4,2048,768]{2,1,0:T(8,128)} copy(f32[4,2048,768]{1,2,0:T(8,128)} %bitcast.185) | data formatting | bytes 50331648 | tf_op jit(solution)/shard_map/reshape | solution.py:59
  821.2 27.0 %copy.101 = f32[4,2048,768]{2,1,0:T(8,128)} copy(f32[4,2048,768]{1,2,0:T(8,128)} %bitcast.184) | data formatting | bytes 50331648 | tf_op jit(solution)/shard_map/reshape | solution.py:59
  856.8 10.8 convolution_bitcast_fusion.1
  867.7 13.2 convolution_bitcast_fusion
  880.8 96.7 %reduce-scatter.3.cloned.1.call-done = f32[4,256,768]{2,1,0:T(8,128)} async-done(((f32[4,2048,768]{2,1,0:T(8,128)}), f32[4,256,768]{2,1,0:T(8,128)}) %reduce-scatter.3.cloned.1.call-update) | async-done | bytes 3145744 | tf_op jit(solution)/shard_map/reduce_scatter | solution.py:237
  980.8 156.6 %reduce-scatter.5.cloned.1.call-done = f32[4,256,768]{2,1,0:T(8,128)} async-done(((f32[4,2048,768]{2,1,0:T(8,128)}), f32[4,256,768]{2,1,0:T(8,128)}) %reduce-scatter.5.cloned.1.call-update) | async-done | bytes 3145744 | tf_op jit(solution)/shard_map/reduce_scatter | solution.py:238
  1141.6 7.2 convolution_bitcast_fusion.2
  1153.1 14.9 add_convert_fusion.1
  1178.6 42.5 %all-reduce = (f32[768]{0:T(1024)}, f32[768]{0:T(1024)}, f32[768]{0:T(1024)}, f32[768]{0:T(1024)}, f32[768]{0:T(1024)}, /*index=5*/f32[768]{0:T(1024)}, f32[768]{0:T(1024)}, f32[3072]{0:T(1024)}, f32[768]{0:T(1024)}) all-reduce(f32[768]{0:T(1024)} %get-tuple-element.258, ...), channel_id=1, replica_groups=mesh['rows'=4,'pos'=8] {'rows','pos'}, use_global_device_ids=true, to_apply=%region_26.27 | all-reduce | flops 9216 | bytes 73728 | tf_op jit(solution)/shard_map/psum | solution.py:251
  1221.1 357.8 %all-reduce.4.cloned.1.call-done = (f32[768,2304]{1,0:T(8,128)}, f32[768,768]{1,0:T(8,128)}, f32[768,3072]{1,0:T(8,128)}, f32[3072,768]{1,0:T(8,128)}) async-done(((f32[768,2304]{1,0:T(8,128)}, f32[768,768]{1,0:T(8,128)}, f32[768,3072]{1,0:T(8,128)}, f32[3072,768]{1,0:T(8,128)}), (f32[768,2304]{1,0:T(8,128)}, f32[768,768]{1,0:T(8,128)}, f32[768,3072]{1,0:T(8,128)}, ...) | async-done | bytes 28311568 | tf_op jit(solution)/shard_map/psum | solution.py:251
  1578.9 6.6 copy.172
  1586.9 9.3 copy.174
  (442 shorter events, 421.4 us)
Async XLA Ops:
  7.2 8.3 copy-start
  7.2 92.1 %all-gather.5.cloned.1.call-start = ((), (), s32[]{:S(2)}) async-start(), calls=%async_computation.3 | async-start | bytes 14155776 | tf_op jit(solution)/shard_map/all_gather | solution.py:130
  7.2 8.3 copy-start.7
  8.1 6.8 copy-start.39
  24.4 149.4 %all-gather.3.cloned.1.call-start = ((), (), s32[]{:S(2)}) async-start(), calls=%async_computation.2 | async-start | bytes 14155776 | tf_op jit(solution)/shard_map/all_gather | solution.py:129
  27.7 949.9 %reduce-scatter.3.cloned.1.call-start = ((), (), s32[]{:S(2)}) async-start(), calls=%async_computation.4 | async-start | bytes 28311552 | tf_op jit(solution)/shard_map/reduce_scatter | solution.py:237
  28.7 336.0 %copy-start.24 = (f32[768]{0:T(1024)}, f32[768]{0:T(1024)S(1)}, u32[]{:S(2)}) copy-start(f32[768]{0:T(1024)S(1)} %convert_element_type.132) | copy-start | bytes 9220
  29.4 302.8 %copy-start.26 = (f32[768]{0:T(1024)}, f32[768]{0:T(1024)S(1)}, u32[]{:S(2)}) copy-start(f32[768]{0:T(1024)S(1)} %convert_element_type.133) | copy-start | bytes 9220
  52.6 7.1 copy-start.54
  189.9 10.7 copy-start.55
  331.6 33.0 %copy-start.3 = (f32[4,256,768]{2,1,0:T(8,128)}, f32[4,256,768]{2,1,0:T(8,128)S(1)}, u32[]{:S(2)}) copy-start(f32[4,256,768]{2,1,0:T(8,128)S(1)} %get-tuple-element.364) | copy-start | bytes 9437188
  331.7 33.0 %copy-start.28 = (f32[4,256]{1,0:T(4,128)}, f32[4,256]{1,0:T(4,128)S(1)}, u32[]{:S(2)}) copy-start(f32[4,256]{1,0:T(4,128)S(1)} %broadcast_multiply_fusion) | copy-start | bytes 12292
  332.2 32.5 %copy-start.30 = (f32[4,256]{1,0:T(4,128)}, f32[4,256]{1,0:T(4,128)S(1)}, u32[]{:S(2)}) copy-start(f32[4,256]{1,0:T(4,128)S(1)} %fusion.92) | copy-start | bytes 12292
  332.2 8.5 copy-start.12
  332.2 8.5 copy-start.50
  358.5 6.1 copy-start.11
  377.7 9.8 copy-start.1
  412.8 9.8 copy-start.1
  447.9 9.8 copy-start.1
  483.1 9.8 copy-start.1
  518.3 9.8 copy-start.1
  553.5 9.8 copy-start.1
  576.4 5.9 copy-start.2
  588.7 9.8 copy-start.1
  611.6 5.9 copy-start.2
  624.0 9.8 copy-start.1
  659.1 9.8 copy-start.1
  694.3 9.8 copy-start.1
  717.1 5.8 copy-start.2
  729.4 9.8 copy-start.1
  752.3 5.9 copy-start.2
  764.7 9.8 copy-start.1
  821.1 316.3 %reduce-scatter.5.cloned.1.call-start = ((), (), s32[]{:S(2)}) async-start(), calls=%async_computation.5 | async-start | bytes 28311552 | tf_op jit(solution)/shard_map/reduce_scatter | solution.py:238
  848.2 730.7 %all-reduce.4.cloned.1.call-start = ((), (), s32[]{:S(2)}) async-start(), calls=%async_computation.6 | async-start | bytes 56623104 | tf_op jit(solution)/shard_map/psum | solution.py:251
  856.8 10.8 copy-start.13
  856.8 10.8 copy-start.51
  977.6 163.9 %copy-start.40 = (f32[768]{0:T(1024)S(1)}, f32[768]{0:T(1024)}, u32[]{:S(2)}) copy-start(f32[768]{0:T(1024)} %copy-done.39) | copy-start | bytes 9220
  977.6 163.9 %copy-start.42 = (f32[4,256]{1,0:T(4,128)S(1)}, f32[4,256]{1,0:T(4,128)}, u32[]{:S(2)}) copy-start(f32[4,256]{1,0:T(4,128)} %copy-done.41) | copy-start | bytes 12292
  977.6 163.9 %copy-start.59 = (f32[768]{0:T(1024)S(1)}, f32[768]{0:T(1024)}, u32[]{:S(2)}) copy-start(f32[768]{0:T(1024)} %copy-done.58) | copy-start | bytes 9220
  980.8 160.7 %copy-start.38 = (f32[4,256]{1,0:T(4,128)S(1)}, f32[4,256]{1,0:T(4,128)}, u32[]{:S(2)}) copy-start(f32[4,256]{1,0:T(4,128)} %copy-done.37) | copy-start | bytes 12292
  1153.1 14.9 copy-start.9
  1153.1 14.9 copy-start.17
  1153.1 14.9 copy-start.20
  1153.1 14.9 copy-start.22
  1578.9 6.6 copy-start.15
  1585.5 10.7 slice-start
  1586.9 9.3 slice-start.1
  1586.9 9.3 slice-start.2
  (83 other events, 267.5 us)
Sparse Core Ops, SparseCore 0:
  24.5 74.7 all-gather.4
  101.8 71.9 all-gather.2
  821.2 156.2 reduce-scatter.2
  981.0 156.3 reduce-scatter.4
  1148.9 429.9 all-reduce.3
where the time goes:
time: 1620 us; the launch traced here: 1610 us
  waiting for transfers between devices  697 us (43%)
  matrix products  514 us (32%)
  local copies, waits for them, and re-layouts  167 us (10%)
  other arithmetic  160 us (10%)
  blocking collectives  53.4 us (3%)
    psum x1, waiting for transfers between devices, per_device(): lax.psum((grad_attn_gain, grad_attn_shift, grad_w_qkv, grad_query_bias, g...  358 us
    dot_general x24, matrix products, head_scores(): jnp.einsum('rqe,rke->rqk', query_head, key_head, preferred_element_type=j...  179 us
    reduce_scatter x1, waiting for transfers between devices, per_device(): lax.psum_scatter(heads_last(value_heads), 'pos', scatter_dimension=1, til...  157 us
    convert_element_type x12, other arithmetic, backward_head(): (probs * (grad_probs - delta_head[..., None])).astype(jnp.bfloat16)  102 us
    reduce_scatter x1, waiting for transfers between devices, per_device(): lax.psum_scatter(heads_last(key_heads), 'pos', scatter_dimension=1, tiled...  96.7 us
    dot_general x12, matrix products, backward_head(): jnp.einsum('rqk,rqe->rke', probs.astype(jnp.bfloat16), grad_head, preferr...  69.7 us
    reshape x3, local copies, waits for them, and re-layouts, heads_last(): values.transpose(1, 2, 0, 3)  54.9 us
    dot_general x12, matrix products, backward_head(): jnp.einsum('rqk,rke->rqe', grad_scores, key_head, preferred_element_type=...  54.6 us
  transfers between devices with their start and end apart: 5, of which 5 were waited for; matrix products, arithmetic and copies ran while one was open for 9% of the time, Pallas kernels for 0%

commit v1 on v0

--- a/solution.py
+++ b/solution.py
@@ -3,6 +3,7 @@
 import jax.numpy as jnp
 from jax import lax
 from jax.sharding import PartitionSpec as P
+from jax.lax import axis_index, axis_size, ppermute
 
 HEAD_DIM = 64
 EPS = 1e-05
@@ -108,6 +109,22 @@
     down_bias,
     cotangent,
 ):
+
+    def balance_sheet(in_array, pos_dim):
+        q_n = axis_size("pos")
+        pool = tuple(((u, (u + 1) % q_n) for u in range(q_n)))
+        pieces_in = tuple(((u, (u - 1) % q_n) for u in range(q_n)))
+        r_now, built = ([in_array], [in_array])
+        for _ in range(q_n // 2):
+            r_now.append(ppermute(r_now[-1], axis_name="pos", perm=pool))
+        for _ in [*range((q_n - 1) // 2)]:
+            built.append(ppermute(built[-1], axis_name="pos", perm=pieces_in))
+        return jnp.roll(
+            jnp.concatenate([*r_now[::-1], *built[1:]], axis=pos_dim),
+            shift=(axis_index("pos") - q_n // 2) * in_array.shape[pos_dim],
+            axis=pos_dim,
+        )
+
     row_count, local_len, model_width = tokens.shape
     row_len = local_len * lax.axis_size("pos")
     score_scale = 1.0 / math.sqrt(HEAD_DIM)
@@ -127,7 +144,7 @@
     segment_wire = segment_ids.astype(jnp.bfloat16)
     keys_all, values_all, segment_all = (
         lax.all_gather(keys_local, "pos", axis=1, tiled=True),
-        lax.all_gather(values_local, "pos", axis=1, tiled=True),
+        balance_sheet(values_local, 1),
         lax.all_gather(segment_wire, "pos", axis=1, tiled=True),
     )
     query_class, query_branch = classes(

time: 1620 us -> 1760 us (1.086)
  waiting for transfers between devices: 697 us -> 765 us
  blocking collectives: 53.4 us -> 93.9 us
  local copies, waits for them, and re-layouts: 167 us -> 197 us
    ppermute x0 -> x7, waiting for transfers between devices: none -> 154 us  [the longest x4 154 us: balance_sheet(): r_now.append(ppermute(r_now[-1], axis_name='pos', perm=pool))]
    all_gather x1, waiting for transfers between devices: 47.4 us -> 0.01 us  [per_device(): lax.all_gather(keys_local, 'pos', axis=1, tiled=True)]
    all_gather x1, blocking collectives: 10.9 us -> 51.3 us  [per_device(): lax.all_gather(segment_wire, 'pos', axis=1, tiled=True)]
    all_gather x1, waiting for transfers between devices: 38.5 us -> 0.01 us  [per_device(): lax.all_gather(values_local, 'pos', axis=1, tiled=True)]
    dynamic_slice x0 -> x2, local copies, waits for them, and re-layouts: none -> 21.2 us  [balance_sheet(): jnp.roll(jnp.concatenate([*r_now[::-1], *built[1:]], axis=pos_dim), shift...]
    unnamed x140 -> x146, local copies, waits for them, and re-layouts: 52.6 us -> 62.2 us
  transfers between devices with their start and end apart: 5 -> 12, of which waited for: 5 -> 6; matrix products, arithmetic and copies ran while one was open for 9% -> 20% of each run, Pallas kernels for 0% -> 0%
where the time goes in v1:
time: 1760 us; the launch traced here: 1750 us
  waiting for transfers between devices  765 us (43%)
  matrix products  514 us (29%)
  local copies, waits for them, and re-layouts  197 us (11%)
  other arithmetic  158 us (9%)
  blocking collectives  93.9 us (5%)
    psum x1, waiting for transfers between devices, per_device(): lax.psum((grad_attn_gain, grad_attn_shift, grad_w_qkv, grad_query_bias, g...  358 us
    dot_general x24, matrix products, head_scores(): jnp.einsum('rqe,rke->rqk', query_head, key_head, preferred_element_type=j...  179 us
    reduce_scatter x1, waiting for transfers between devices, per_device(): lax.psum_scatter(heads_last(value_heads), 'pos', scatter_dimension=1, til...  156 us
    ppermute x4, waiting for transfers between devices, balance_sheet(): r_now.append(ppermute(r_now[-1], axis_name='pos', perm=pool))  154 us
    convert_element_type x12, other arithmetic, backward_head(): (probs * (grad_probs - delta_head[..., None])).astype(jnp.bfloat16)  102 us
    reduce_scatter x1, waiting for transfers between devices, per_device(): lax.psum_scatter(heads_last(key_heads), 'pos', scatter_dimension=1, tiled...  96.3 us
    dot_general x12, matrix products, backward_head(): jnp.einsum('rqk,rqe->rke', probs.astype(jnp.bfloat16), grad_head, preferr...  69.6 us
    unnamed x146, local copies, waits for them, and re-layouts  62.2 us
  transfers between devices with their start and end apart: 12, of which 6 were waited for; matrix products, arithmetic and copies ran while one was open for 20% of the time, Pallas kernels for 0%

profile of v1, /device:TPU:0, one launch (start us, length us, event | category | flops | bytes accessed | tf_op | source)
XLA Modules:
  0.0 1752.6 jit_solution(18382342704667441326)
XLA Ops:
  28.5 38.1 %collective-permute-done = bf16[4,256,768]{2,1,0:T(8,128)(2,1)} collective-permute-done((bf16[4,256,768]{2,1,0:T(8,128)(2,1)}, bf16[4,256,768]{2,1,0:T(8,128)(2,1)}, u32[]{:S(2)}, u32[]{:S(2)}) %collective-permute-start) | collective-permute-done | bytes 1572896 | tf_op jit(solution)/shard_map/ppermute | solution.py:119
  71.0 66.5 %collective-permute-done.1 = bf16[4,256,768]{2,1,0:T(8,128)(2,1)} collective-permute-done((bf16[4,256,768]{2,1,0:T(8,128)(2,1)}, bf16[4,256,768]{2,1,0:T(8,128)(2,1)}, u32[]{:S(2)}, u32[]{:S(2)}) %collective-permute-start.1) | collective-permute-done | bytes 1572896 | tf_op jit(solution)/shard_map/ppermute | solution.py:119
  143.9 51.3 %all_gather.11 = bf16[4,2048]{1,0:T(4,128)(2,1)S(1)} all-gather(bf16[4,256]{1,0:T(4,128)(2,1)S(1)} %get-tuple-element.361), channel_id=1, replica_groups=mesh['rows'=4,'pos'=8] {'pos'}, dimensions={1}, use_global_device_ids=true | all-gather | bytes 18432 | tf_op jit(solution)/shard_map/all_gather | solution.py:148
  211.2 49.6 %collective-permute-done.3 = bf16[4,256,768]{2,1,0:T(8,128)(2,1)} collective-permute-done((bf16[4,256,768]{2,1,0:T(8,128)(2,1)}, bf16[4,256,768]{2,1,0:T(8,128)(2,1)}, u32[]{:S(2)}, u32[]{:S(2)}) %collective-permute-start.3) | collective-permute-done | bytes 1572896 | tf_op jit(solution)/shard_map/ppermute | solution.py:119
  287.9 15.6 copy.83
  303.5 16.7 copy.82
  320.2 10.7 copy.89
  330.9 127.0 %while.30 = (s32[]{:T(128)}, bf16[12,4,256,64]{2,3,0,1:T(8,128)(2,1)}, f32[12,4,256]{2,1,0:T(4,128)}, f32[12,4,256]{2,1,0:T(4,128)}, bf16[12,4,256,64]{2,3,1,0:T...) while((s32[]{:T(128)}, ...), condition=%wide.region_13.14_spmd.clone, body=%wide.region_10.13_spmd.clone.sunk | while | flops 564131840 | bytes 28301456 | solution.py:177
  462.6 8.5 fusion.65
  471.2 17.8 %convert_reduce_fusion = (f32[3072]{0:T(1024)}, bf16[4,256,3072]{2,1,0:T(8,128)(2,1)S(1)}) fusion(bf16[4,256,768]{2,1,0:T(8,128)(2,1)S(1)} %copy-done.13, bf16[3072,768]{1,0:T(8,128)(2,1)} %param.41, f32[4,256,3072]{2,1,0:T(8,128)} %fusion.65, f32[3072]{0:T(1024)S(1)} %copy-done.46), kind=kOutput, calls=%fused_computation.65 | convolution fusion | flops 4916769792 | bytes 25190400 | tf_op jit(solution)/shard_map/rpo,io->rpi/dot_general | solution.py:83
  504.6 16.7 copy.94
  521.3 421.6 %while.31 = (s32[]{:T(128)}, bf16[12,4,256,64]{2,3,0,1:T(8,128)(2,1)}, f32[12,4,2048,64]{2,3,0,1:T(8,128)}, f32[12,4,2048,64]{2,3,0,1:T(8,128)}, bf16[12,4,256,6...) while((s32[]{:T(128)}, ...), condition=%wide.region_20.21_spmd.clone, body=%wide.region_18.20_spmd.clone.sunk | while | flops 1374288896 | bytes 124245304 | solution.py:242
  524.7 9.8 multiply_reduce_fusion.5
  534.5 8.5 multiply_convert_fusion.5
  559.8 9.8 multiply_reduce_fusion.5
  569.6 8.5 multiply_convert_fusion.5
  594.9 9.8 multiply_reduce_fusion.5
  604.6 8.5 multiply_convert_fusion.5
  629.9 9.8 multiply_reduce_fusion.5
  639.7 8.5 multiply_convert_fusion.5
  665.1 9.8 multiply_reduce_fusion.5
  674.9 8.5 multiply_convert_fusion.5
  700.3 9.8 multiply_reduce_fusion.5
  710.0 8.5 multiply_convert_fusion.5
  735.4 9.8 multiply_reduce_fusion.5
  745.2 8.5 multiply_convert_fusion.5
  770.7 9.8 multiply_reduce_fusion.5
  780.5 8.5 multiply_convert_fusion.5
  805.8 9.8 multiply_reduce_fusion.5
  815.6 8.5 multiply_convert_fusion.5
  840.9 9.8 multiply_reduce_fusion.5
  850.7 8.5 multiply_convert_fusion.5
  876.0 9.8 multiply_reduce_fusion.5
  885.8 8.5 multiply_convert_fusion.5
  911.3 9.8 multiply_reduce_fusion.5
  921.1 8.5 multiply_convert_fusion.5
  943.0 24.7 %copy.101 = f32[4,2048,768]{2,1,0:T(8,128)} copy(f32[4,2048,768]{1,2,0:T(8,128)} %bitcast.192) | data formatting | bytes 50331648 | tf_op jit(solution)/shard_map/reshape | solution.py:60
  967.7 26.9 %copy.103 = f32[4,2048,768]{2,1,0:T(8,128)} copy(f32[4,2048,768]{1,2,0:T(8,128)} %bitcast.191) | data formatting | bytes 50331648 | tf_op jit(solution)/shard_map/reshape | solution.py:60
  1003.0 10.8 convolution_bitcast_fusion.1
  1013.8 13.2 convolution_bitcast_fusion
  1027.0 96.3 %reduce-scatter.3.cloned.1.call-done = f32[4,256,768]{2,1,0:T(8,128)} async-done(((f32[4,2048,768]{2,1,0:T(8,128)}), f32[4,256,768]{2,1,0:T(8,128)}) %reduce-scatter.3.cloned.1.call-update) | async-done | bytes 3145744 | tf_op jit(solution)/shard_map/reduce_scatter | solution.py:254
  1126.6 156.5 %reduce-scatter.5.cloned.1.call-done = f32[4,256,768]{2,1,0:T(8,128)} async-done(((f32[4,2048,768]{2,1,0:T(8,128)}), f32[4,256,768]{2,1,0:T(8,128)}) %reduce-scatter.5.cloned.1.call-update) | async-done | bytes 3145744 | tf_op jit(solution)/shard_map/reduce_scatter | solution.py:255
  1287.2 7.2 convolution_bitcast_fusion.2
  1298.8 14.9 add_convert_fusion.1
  1324.2 42.5 %all-reduce = (f32[768]{0:T(1024)}, f32[768]{0:T(1024)}, f32[768]{0:T(1024)}, f32[768]{0:T(1024)}, f32[768]{0:T(1024)}, /*index=5*/f32[768]{0:T(1024)}, f32[768]{0:T(1024)}, f32[3072]{0:T(1024)}, f32[768]{0:T(1024)}) all-reduce(f32[768]{0:T(1024)} %get-tuple-element.258, ...), channel_id=1, replica_groups=mesh['rows'=4,'pos'=8] {'rows','pos'}, use_global_device_ids=true, to_apply=%region_26.27 | all-reduce | flops 9216 | bytes 73728 | tf_op jit(solution)/shard_map/psum | solution.py:268
  1366.8 357.8 %all-reduce.4.cloned.1.call-done = (f32[768,2304]{1,0:T(8,128)}, f32[768,768]{1,0:T(8,128)}, f32[768,3072]{1,0:T(8,128)}, f32[3072,768]{1,0:T(8,128)}) async-done(((f32[768,2304]{1,0:T(8,128)}, f32[768,768]{1,0:T(8,128)}, f32[768,3072]{1,0:T(8,128)}, f32[3072,768]{1,0:T(8,128)}), (f32[768,2304]{1,0:T(8,128)}, f32[768,768]{1,0:T(8,128)}, f32[768,3072]{1,0:T(8,128)}, ...) | async-done | bytes 28311568 | tf_op jit(solution)/shard_map/psum | solution.py:268
  1724.5 6.6 copy.191
  1732.5 9.3 copy.193
  (465 shorter events, 459.2 us)
Async XLA Ops:
  7.2 296.3 %all-gather.3.cloned.1.call-start = ((), (), s32[]{:S(2)}) async-start(), calls=%async_computation.2 | async-start | bytes 14155776 | tf_op jit(solution)/shard_map/all_gather | solution.py:146
  8.1 9.6 copy-start.35
  22.8 481.8 %all-gather.5.cloned.1.call-start = ((), (), s32[]{:S(2)}) async-start(), calls=%async_computation.3 | async-start | bytes 14155776 | tf_op jit(solution)/shard_map/all_gather | solution.py:213
  22.9 46.5 %copy-start.60 = (s32[4,2]{0,1:T(2,128)S(1)}, s32[4,2]{0,1:T(2,128)}, u32[]{:S(2)}) copy-start(s32[4,2]{0,1:T(2,128)} %param.26) | copy-start | bytes 100
  22.9 46.5 %copy-start.55 = (s32[4,2,16]{2,1,0:T(2,128)S(1)}, s32[4,2,16]{2,1,0:T(2,128)}, u32[]{:S(2)}) copy-start(s32[4,2,16]{2,1,0:T(2,128)} %param.28) | copy-start | bytes 1540
  22.9 114.6 %copy-start.48 = (s32[4,2]{0,1:T(2,128)S(1)}, s32[4,2]{0,1:T(2,128)}, u32[]{:S(2)}) copy-start(s32[4,2]{0,1:T(2,128)} %param.27) | copy-start | bytes 100
  28.0 38.6 %collective-permute-start = (bf16[4,256,768]{2,1,0:T(8,128)(2,1)}, bf16[4,256,768]{2,1,0:T(8,128)(2,1)}, u32[]{:S(2)}, u32[]{:S(2)}) collective-permute-start(bf16[4,256,768]{2,1,0:T(8,128)(2,1)} %get-tuple-element.356), channel_id=1, source_target_pairs={{0,1},{1,2},{2,3},{3,4},{4,5},{5,6},{6,7},{7,0},{8,9},{9,10},{10,1... | collective-permute-start | bytes 4718600 | tf_op jit(solution)/shard_map/ppermute | solution.py:119
  66.6 70.9 %collective-permute-start.1 = (bf16[4,256,768]{2,1,0:T(8,128)(2,1)}, bf16[4,256,768]{2,1,0:T(8,128)(2,1)}, u32[]{:S(2)}, u32[]{:S(2)}) collective-permute-start(bf16[4,256,768]{2,1,0:T(8,128)(2,1)} %collective-permute-done), channel_id=1, source_target_pairs={{0,1},{1,2},{2,3},{3,4},{4,5},{5,6},{6,7},{7,0},{8,9},{9,10},{10,1... | collective-permute-start | bytes 4718600 | tf_op jit(solution)/shard_map/ppermute | solution.py:119
  66.6 73.1 %collective-permute-start.4 = (bf16[4,256,768]{2,1,0:T(8,128)(2,1)}, bf16[4,256,768]{2,1,0:T(8,128)(2,1)}, u32[]{:S(2)}, u32[]{:S(2)}) collective-permute-start(bf16[4,256,768]{2,1,0:T(8,128)(2,1)} %get-tuple-element.356), channel_id=1, source_target_pairs={{0,7},{1,0},{2,1},{3,2},{4,3},{5,4},{6,5},{7,6},{8,15},{9,8},{10,9... | collective-permute-start | bytes 4718600 | tf_op jit(solution)/shard_map/ppermute | solution.py:121
  69.3 1053.9 %reduce-scatter.3.cloned.1.call-start = ((), (), s32[]{:S(2)}) async-start(), calls=%async_computation.4 | async-start | bytes 28311552 | tf_op jit(solution)/shard_map/reduce_scatter | solution.py:254
  137.5 58.6 %collective-permute-start.2 = (bf16[4,256,768]{2,1,0:T(8,128)(2,1)}, bf16[4,256,768]{2,1,0:T(8,128)(2,1)}, u32[]{:S(2)}, u32[]{:S(2)}) collective-permute-start(bf16[4,256,768]{2,1,0:T(8,128)(2,1)} %collective-permute-done.1), channel_id=1, source_target_pairs={{0,1},{1,2},{2,3},{3,4},{4,5},{5,6},{6,7},{7,0},{8,9},{9,10},{10,1... | collective-permute-start | bytes 4718600 | tf_op jit(solution)/shard_map/ppermute | solution.py:119
  139.0 56.3 %copy-start.50 = (s32[256]{0:T(256)}, s32[256]{0:T(256)S(1)}, u32[]{:S(2)}) copy-start(s32[256]{0:T(256)S(1)} %iota_add_fusion) | copy-start | bytes 3076
  139.7 57.9 %collective-permute-start.5 = (bf16[4,256,768]{2,1,0:T(8,128)(2,1)}, bf16[4,256,768]{2,1,0:T(8,128)(2,1)}, u32[]{:S(2)}, u32[]{:S(2)}) collective-permute-start(bf16[4,256,768]{2,1,0:T(8,128)(2,1)} %collective-permute-done.4), channel_id=1, source_target_pairs={{0,7},{1,0},{2,1},{3,2},{4,3},{5,4},{6,5},{7,6},{8,15},{9,8},{10,9... | collective-permute-start | bytes 4718600 | tf_op jit(solution)/shard_map/ppermute | solution.py:121
  196.1 64.6 %collective-permute-start.3 = (bf16[4,256,768]{2,1,0:T(8,128)(2,1)}, bf16[4,256,768]{2,1,0:T(8,128)(2,1)}, u32[]{:S(2)}, u32[]{:S(2)}) collective-permute-start(bf16[4,256,768]{2,1,0:T(8,128)(2,1)} %collective-permute-done.2), channel_id=1, source_target_pairs={{0,1},{1,2},{2,3},{3,4},{4,5},{5,6},{6,7},{7,0},{8,9},{9,10},{10,1... | collective-permute-start | bytes 4718600 | tf_op jit(solution)/shard_map/ppermute | solution.py:119
  197.6 72.5 %collective-permute-start.6 = (bf16[4,256,768]{2,1,0:T(8,128)(2,1)}, bf16[4,256,768]{2,1,0:T(8,128)(2,1)}, u32[]{:S(2)}, u32[]{:S(2)}) collective-permute-start(bf16[4,256,768]{2,1,0:T(8,128)(2,1)} %collective-permute-done.5), channel_id=1, source_target_pairs={{0,7},{1,0},{2,1},{3,2},{4,3},{5,4},{6,5},{7,6},{8,15},{9,8},{10,9... | collective-permute-start | bytes 4718600 | tf_op jit(solution)/shard_map/ppermute | solution.py:121
  201.4 293.7 %copy-start.25 = (f32[768]{0:T(1024)}, f32[768]{0:T(1024)S(1)}, u32[]{:S(2)}) copy-start(f32[768]{0:T(1024)S(1)} %convert_element_type.132) | copy-start | bytes 9220
  202.1 260.4 %copy-start.27 = (f32[768]{0:T(1024)}, f32[768]{0:T(1024)S(1)}, u32[]{:S(2)}) copy-start(f32[768]{0:T(1024)S(1)} %convert_element_type.133) | copy-start | bytes 9220
  320.2 10.7 copy-start.52
  462.0 33.1 %copy-start.3 = (f32[4,256,768]{2,1,0:T(8,128)}, f32[4,256,768]{2,1,0:T(8,128)S(1)}, u32[]{:S(2)}) copy-start(f32[4,256,768]{2,1,0:T(8,128)S(1)} %get-tuple-element.364) | copy-start | bytes 9437188
  462.1 33.1 %copy-start.29 = (f32[4,256]{1,0:T(4,128)}, f32[4,256]{1,0:T(4,128)S(1)}, u32[]{:S(2)}) copy-start(f32[4,256]{1,0:T(4,128)S(1)} %broadcast_multiply_fusion) | copy-start | bytes 12292
  462.6 32.5 %copy-start.31 = (f32[4,256]{1,0:T(4,128)}, f32[4,256]{1,0:T(4,128)S(1)}, u32[]{:S(2)}) copy-start(f32[4,256]{1,0:T(4,128)S(1)} %fusion.92) | copy-start | bytes 12292
  504.6 16.7 copy-start.56
  504.6 16.7 copy-start.57
  524.7 9.8 copy-start.1
  559.8 9.8 copy-start.1
  594.8 9.8 copy-start.1
  629.9 9.8 copy-start.1
  665.1 9.8 copy-start.1
  700.2 9.8 copy-start.1
  735.4 9.8 copy-start.1
  770.7 9.8 copy-start.1
  805.8 9.8 copy-start.1
  840.9 9.8 copy-start.1
  876.0 9.8 copy-start.1
  911.3 9.8 copy-start.1
  967.7 315.4 %reduce-scatter.5.cloned.1.call-start = ((), (), s32[]{:S(2)}) async-start(), calls=%async_computation.5 | async-start | bytes 28311552 | tf_op jit(solution)/shard_map/reduce_scatter | solution.py:255
  994.7 729.8 %all-reduce.4.cloned.1.call-start = ((), (), s32[]{:S(2)}) async-start(), calls=%async_computation.6 | async-start | bytes 56623104 | tf_op jit(solution)/shard_map/psum | solution.py:268
  1002.9 10.8 copy-start.14
  1003.0 10.8 copy-start.47
  1123.2 163.9 %copy-start.36 = (f32[768]{0:T(1024)S(1)}, f32[768]{0:T(1024)}, u32[]{:S(2)}) copy-start(f32[768]{0:T(1024)} %copy-done.35) | copy-start | bytes 9220
  1123.2 163.9 %copy-start.38 = (f32[4,256]{1,0:T(4,128)S(1)}, f32[4,256]{1,0:T(4,128)}, u32[]{:S(2)}) copy-start(f32[4,256]{1,0:T(4,128)} %copy-done.37) | copy-start | bytes 12292
  1123.2 163.9 %copy-start.54 = (f32[768]{0:T(1024)S(1)}, f32[768]{0:T(1024)}, u32[]{:S(2)}) copy-start(f32[768]{0:T(1024)} %copy-done.53) | copy-start | bytes 9220
  1126.6 160.6 %copy-start.34 = (f32[4,256]{1,0:T(4,128)S(1)}, f32[4,256]{1,0:T(4,128)}, u32[]{:S(2)}) copy-start(f32[4,256]{1,0:T(4,128)} %copy-done.33) | copy-start | bytes 12292
  1298.8 14.9 copy-start.9
  1298.8 14.9 copy-start.18
  1298.8 14.9 copy-start.21
  1298.8 14.9 copy-start.23
  1731.1 10.7 slice-start
  (86 other events, 332.7 us)
Sparse Core Ops, SparseCore 0:
  22.9 114.5 all-gather.2
  140.0 114.3 all-gather.4
  967.8 155.3 reduce-scatter.2
  1126.7 156.3 reduce-scatter.4
  1294.5 429.9 all-reduce.3
